TPU v7x, 32 devices: a whole 2x2x4 slice. The times are simulated.
32 devices in a mesh: tm: 16 (over z, y, core), series: 2 (over x).
Axes of the slice: x: 2, y: 2, z: 4, core: 2. Of those that a mesh axis runs over, the one named last changes fastest.
Arguments:
- panel: bfloat16 [4096, 16384], P('series', 'tm'), may hold values from -6 to 6
- series_factors: bfloat16 [4096, 128], P('series'), may hold values from -1.796875 to 1.796875
- time_factors: bfloat16 [16384, 128], P('tm'), may hold values from -1.796875 to 1.796875
- ar_weights: float32 [16, 128], replicated, may hold values from -1 to 1
- tile_mask: int32 [32, 128], P('series', 'tm'), may hold values 0 or 1
- lags: int32 [16], replicated, may hold values from 1 to 128, as said below
Outputs:
- series_grad: float32 [4096, 128], P(('series', 'tm'))
- time_grad: float32 [16384, 128], P(('tm', 'series'))
- ar_grad: float32 [16, 128], replicated
Inputs may be any that keep to these rules, and one draw needn't show every extreme that they name: `lags`: strictly increasing, and the last equals 128.
All inputs are finite; a program needn't handle non-finite values. No bound on the sum of `tile_mask` on one device may be relied on, other than what follows from the above.
Results may differ from a plain program's by a relative error of at most 0.00045.
Values may be sent and summed in bfloat16 or wider, within the bound.
A program may use at most 64 MiB of HBM per device.

v0:
```python
import math

import jax
import jax.numpy as jnp
from jax import lax
from jax.sharding import PartitionSpec as P

NLAG = 16
LAGMAX = 128
TILE = 128


ar_strength = 1.0


def from_behind(value, axis, steps):
    count = lax.axis_size(axis)
    initial, last = (max(0, -steps), min(count, count - steps))
    return lax.ppermute(value, axis, [(source, source + steps) for source in range(initial, last)])


def lag_error(extended, weights, lags, count):
    total = extended[LAGMAX : LAGMAX + count]
    for lag_pos in range(NLAG):
        shifted = lax.dynamic_slice_in_dim(extended, LAGMAX - lags[lag_pos], count, 0)
        total = total - weights[lag_pos] * shifted
    return total


def per_device(panel, series_factors, time_factors, ar_weights, tile_mask, lags):
    time_rows = time_factors.shape[0]
    series_rows = series_factors.shape[0]
    time_devices = lax.axis_size("tm")
    series_devices = lax.axis_size("series")
    scale_time = 1.0 / math.sqrt(time_rows * time_devices)
    scale_series = 1.0 / math.sqrt(series_rows * series_devices)
    tm_index = lax.axis_index("tm")
    earlier = from_behind(time_factors[time_rows - LAGMAX :], "tm", 1)
    keep = jnp.repeat(jnp.repeat(tile_mask, TILE, 0), TILE, 1) > 0
    predicted = jnp.dot(series_factors, time_factors.T, preferred_element_type=jnp.float32)
    residual = jnp.where(keep, predicted - panel.astype(jnp.float32), jnp.float32(0.0)).astype(
        jnp.bfloat16
    )
    series_part = jnp.dot(residual, time_factors, preferred_element_type=jnp.float32) * scale_time
    time_part = (
        lax.dot_general(
            residual, series_factors, (((0,), (0,)), ((), ())), preferred_element_type=jnp.float32
        )
        * scale_series
    )
    factors32 = time_factors.astype(jnp.float32)
    extended = jnp.concatenate([earlier.astype(jnp.float32), factors32], axis=0)
    moments = tm_index * time_rows + jnp.arange(time_rows, dtype=jnp.int32)
    error = jnp.where(
        (moments >= LAGMAX)[:, None],
        lag_error(extended, ar_weights, lags, time_rows),
        jnp.float32(0.0),
    )
    upcoming = from_behind(error[:LAGMAX].astype(jnp.bfloat16), "tm", -1).astype(jnp.float32)
    error_ext = jnp.concatenate([error, upcoming], axis=0)
    adjoint = error
    ar_rows = []
    for lag_pos in range(NLAG):
        ahead = lax.dynamic_slice_in_dim(error_ext, lags[lag_pos], time_rows, 0)
        adjoint = adjoint - ar_weights[lag_pos] * ahead
        behind = lax.dynamic_slice_in_dim(extended, LAGMAX - lags[lag_pos], time_rows, 0)
        ar_rows.append(-scale_time * jnp.sum(error * behind, axis=0))
    ar_part = jnp.stack(ar_rows)
    series_grad = lax.psum_scatter(series_part, "tm", scatter_dimension=0, tiled=True)
    ar_grad = lax.psum(ar_part, "tm")
    time_share = lax.psum_scatter(time_part, "series", scatter_dimension=0, tiled=True)
    own_time = time_rows // series_devices
    adjoint_rows = lax.dynamic_slice_in_dim(
        adjoint, lax.axis_index("series") * own_time, own_time, 0
    )
    time_grad = time_share + ar_strength * adjoint_rows
    return (series_grad, time_grad, ar_grad)


def solution(mesh):
    in_specs = (P("series", "tm"), P("series", None), P("tm", None), P(), P("series", "tm"), P())
    out_specs = (P(("series", "tm"), None), P(("tm", "series"), None), P())
    return jax.shard_map(
        per_device, mesh=mesh, in_specs=in_specs, out_specs=out_specs, check_vma=False
    )
```

profile of v0, /device:TPU:0, one launch (start us, length us, event | category | flops | bytes accessed | tf_op | source)
XLA Modules:
  0.0 137.6 jit_solution(11205370588736498086)
XLA Ops:
  7.2 0.0 copy-start
  7.2 0.0 reduce-scatter.5.cloned.1.call-start
  7.2 0.7 broadcast_compare_fusion
  8.0 0.1 copy.9
  8.1 0.1 broadcast_in_dim.23
  8.1 6.4 %broadcast_in_dim.24 = pred[2048,8,128]{2,1,0:T(8,128)(4,1)S(1)} broadcast(pred[2048,8]{1,0:T(8,128)(4,1)S(1)} %bitcast.91), dimensions={0,1} | broadcast | bytes 2113536 | tf_op jit(solution)/shard_map/broadcast_in_dim | solution.py:39
  14.5 0.0 copy-done
  14.5 4.1 %select_convert_fusion = bf16[2048,1024]{1,0:T(8,128)(2,1)S(1)} fusion(bf16[2048,1024]{1,0:T(8,128)(2,1)} %param.6, pred[256,8,8,128]{3,2,1,0:T(8,128)(4,1)S(1)} %bitcast.90, bf16[2048,128]{1,0:T(8,128)(2,1)S(1)} %copy-done, bf16[1024,128]{1,0:T(8,128)(2,1)} %param.8), kind=kOutput, calls=%fused_computation | convolution fusion | flops 545259520 | bytes 11272192 | tf_op jit(solution)/shard_map/dot_general | solution.py:40
  18.6 0.0 copy-start.1
  18.6 1.9 %copy-done.1 = bf16[2048,1024]{1,0:T(8,128)(2,1)} copy-done((bf16[2048,1024]{1,0:T(8,128)(2,1)}, bf16[2048,1024]{1,0:T(8,128)(2,1)S(1)}, u32[]{:S(2)}) %copy-start.1) | copy-done | bytes 4194328
  20.5 2.1 %convolution_multiply_fusion.1 = f32[1024,128]{1,0:T(8,128)} fusion(bf16[2048,1024]{1,0:T(8,128)(2,1)S(1)} %select_convert_fusion, bf16[2048,128]{1,0:T(8,128)(2,1)S(1)} %copy-done), kind=kOutput, calls=%fused_computation.34 | convolution fusion | flops 537001984 | bytes 5242880 | tf_op jit(solution)/shard_map/dot_general | solution.py:46
  22.6 0.0 reduce-scatter.5.cloned.1.call-update
  22.6 0.0 reduce-scatter.3.cloned.1.call-start
  22.7 0.0 copy-done.2
  22.7 2.4 %collective-permute-start = (bf16[128,128]{1,0:T(8,128)(2,1)S(1)}, bf16[128,128]{1,0:T(8,128)(2,1)S(1)}, u32[]{:S(2)}, u32[]{:S(2)}) collective-permute-start(bf16[128,128]{1,0:T(8,128)(2,1)S(1)} %slice.70), channel_id=1, source_target_pairs={{0,2},{2,4},{4,6},{6,8},{8,10},{10,12},{12,14},{14,16},{16,18},{18... | collective-permute-start | bytes 98312 | tf_op jit(solution)/shard_map/ppermute | solution.py:19
  25.1 4.4 %convolution_multiply_fusion = f32[2048,128]{1,0:T(8,128)} fusion(bf16[2048,1024]{1,0:T(8,128)(2,1)} %copy-done.1, bf16[1024,128]{1,0:T(8,128)(2,1)S(1)} %copy-done.2), kind=kOutput, calls=%fused_computation.33 | convolution fusion | flops 537133056 | bytes 5505024 | tf_op jit(solution)/shard_map/dot_general | solution.py:44
  29.5 0.0 reduce-scatter.3.cloned.1.call-update
  29.6 0.0 copy-done.3
  29.6 0.7 fusion.63
  30.3 0.0 copy-done.4
  80.7 0.0 collective-permute-done
  80.7 4.1 %multiply_reduce_fusion = (f32[128]{0:T(128)S(1)}, f32[128]{0:T(128)S(1)}, f32[128]{0:T(128)S(1)}, f32[128]{0:T(128)S(1)}, f32[128]{0:T(128)S(1)}, /*index=5*/f32[128]{0:T(128)S(1)}, f32[1024,128]{1,0:T(8,128)S(1)}) fusion(s32[]{:T(128)S(6)} %select_n.139, f32[1024,128]{1,0:T(8,128)S(1)} %convert_element_type.18, f32[128,128]{1,0:T(8,128)S(1)} %convert_element_type.19, ...), kind=kLoop, calls=%fused_computation.116 | loop fusion | flops 8912128 | bytes 1388608 | tf_op jit(solution)/shard_map/reduce_sum | solution.py:67
  84.8 0.5 multiply_reduce_fusion.12
  85.3 0.7 multiply_reduce_fusion.6
  86.0 1.3 collective-permute-start.1
  87.4 0.1 stack.2
  87.5 37.2 %psum.7 = f32[16,128]{1,0:T(8,128)} all-reduce(f32[16,128]{1,0:T(8,128)S(1)} %stack.2), channel_id=1, replica_groups=mesh['tm'=16,'series'=2] {'tm'}, use_global_device_ids=true, to_apply=%region_18.19 | all-reduce | flops 2048 | bytes 16384 | tf_op jit(solution)/shard_map/psum | solution.py:70
  124.6 0.0 collective-permute-done.1
  124.6 0.5 fusion.31
  125.2 3.3 %fusion.11 = f32[1024,128]{1,0:T(8,128)S(1)} fusion(f32[1024,128]{1,0:T(8,128)S(1)} %get-tuple-element.19, s32[]{:T(128)S(6)} %select_n.141, s32[]{:T(128)S(6)} %select_n.142, s32[]{:T(128)S(6)} %select_n.143, s32[]{:T(128)S(6)} %select_n.144, s32[]{:T(128)S(6)} %select_n.145, s32[]{:T(128)S(6)} %select_n.146, s32[]{:T(128)S(6)} %select_n.147, ...), kind=kLoop, calls=%fused_computation.78 | loop fusion | flops 3932160 | bytes 1119272 | tf_op jit(solution)/shard_map/sub | solution.py:65
  128.4 0.0 reduce-scatter.5.cloned.1.call-done
  128.5 2.2 %fusion.52 = f32[512,128]{1,0:T(8,128)} fusion(f32[512,128]{1,0:T(8,128)} %reduce-scatter.5.cloned.1.call-done, s32[]{:T(128)S(6)} %add.192, f32[1024,128]{1,0:T(8,128)S(1)} %get-tuple-element.19, s32[]{:T(128)S(6)} %add.186, s32[]{:T(128)S(6)} %add.188, s32[]{:T(128)S(6)} %add.190, f32[128,128]{1,0:T(8,128)S(1)} %convert_element_type.20, ...), kind=kLoop, calls=%fused_computation.136 | loop fusion | flops 1048576 | bytes 1903124 | tf_op jit(solution)/shard_map/add | solution.py:76
  (19 shorter events, 0.1 us)
Async XLA Ops:
  7.2 7.3 %copy-start = (bf16[2048,128]{1,0:T(8,128)(2,1)S(1)}, bf16[2048,128]{1,0:T(8,128)(2,1)}, u32[]{:S(2)}) copy-start(bf16[2048,128]{1,0:T(8,128)(2,1)} %param.7) | copy-start | bytes 1572868
  7.2 121.3 %reduce-scatter.5.cloned.1.call-start = ((), (), s32[]{:S(2)}) async-start(), calls=%async_computation.3 | async-start | bytes 786432 | tf_op jit(solution)/shard_map/reduce_scatter | solution.py:71
  18.6 1.9 %copy-start.1 = (bf16[2048,1024]{1,0:T(8,128)(2,1)}, bf16[2048,1024]{1,0:T(8,128)(2,1)S(1)}, u32[]{:S(2)}) copy-start(bf16[2048,1024]{1,0:T(8,128)(2,1)S(1)} %select_convert_fusion) | copy-start | bytes 12582916
  20.5 2.2 %copy-start.2 = (bf16[1024,128]{1,0:T(8,128)(2,1)S(1)}, bf16[1024,128]{1,0:T(8,128)(2,1)}, u32[]{:S(2)}) copy-start(bf16[1024,128]{1,0:T(8,128)(2,1)} %param.8) | copy-start | bytes 786436
  22.6 7.0 %copy-start.3 = (s32[16]{0:T(128)S(1)}, s32[16]{0:T(128)}, u32[]{:S(2)}) copy-start(s32[16]{0:T(128)} %param.11) | copy-start | bytes 196
  22.6 7.7 %copy-start.4 = (f32[16,128]{1,0:T(8,128)S(1)}, f32[16,128]{1,0:T(8,128)}, u32[]{:S(2)}) copy-start(f32[16,128]{1,0:T(8,128)} %param.9) | copy-start | bytes 24580
  22.6 108.1 %reduce-scatter.3.cloned.1.call-start = ((), (), s32[]{:S(2)}) async-start(), calls=%async_computation.2 | async-start | bytes 1114112 | tf_op jit(solution)/shard_map/reduce_scatter | solution.py:69
  22.7 58.0 %collective-permute-start = (bf16[128,128]{1,0:T(8,128)(2,1)S(1)}, bf16[128,128]{1,0:T(8,128)(2,1)S(1)}, u32[]{:S(2)}, u32[]{:S(2)}) collective-permute-start(bf16[128,128]{1,0:T(8,128)(2,1)S(1)} %slice.70), channel_id=1, source_target_pairs={{0,2},{2,4},{4,6},{6,8},{8,10},{10,12},{12,14},{14,16},{16,18},{18... | collective-permute-start | bytes 98312 | tf_op jit(solution)/shard_map/ppermute | solution.py:19
  86.0 38.6 %collective-permute-start.1 = (bf16[128,128]{1,0:T(8,128)(2,1)S(1)}, bf16[128,128]{1,0:T(8,128)(2,1)S(1)}, u32[]{:S(2)}, u32[]{:S(2)}) collective-permute-start(bf16[128,128]{1,0:T(8,128)(2,1)S(1)} %slice.203), channel_id=1, source_target_pairs={{2,0},{4,2},{6,4},{8,6},{10,8},{12,10},{14,12},{16,14},{18,16},{20... | collective-permute-start | bytes 98312 | tf_op jit(solution)/shard_map/ppermute | solution.py:19
Sparse Core Ops, SparseCore 0:
  22.8 17.3 reduce-scatter.4
  44.3 57.6 reduce-scatter.2
where the time goes:
time: 139 us; the launch traced here: 138 us
  between operations  64.6 us (46%)
  blocking collectives  37.2 us (27%)
  other arithmetic  12.2 us (9%)
  matrix products  10.6 us (8%)
  local copies, waits for them, and re-layouts  9.25 us (7%)
  starting transfers between devices  3.77 us (3%)
    psum x1, blocking collectives, per_device(): ar_grad = lax.psum(ar_part, 'tm')  37.2 us
    broadcast_in_dim x2, local copies, waits for them, and re-layouts, per_device(): keep = jnp.repeat(jnp.repeat(tile_mask, TILE, 0), TILE, 1) > 0  6.44 us
    reduce_sum x3, other arithmetic, per_device(): ar_rows.append(-scale_time * jnp.sum(error * behind, axis=0))  5.29 us
    dot_general x1, matrix products, per_device(): jnp.dot(residual, time_factors, preferred_element_type=jnp.float32)  4.42 us
    dot_general x1, matrix products, per_device(): jnp.dot(series_factors, time_factors.T, preferred_element_type=jnp.float32)  4.07 us
    ppermute x2, starting transfers between devices, from_behind(): lax.ppermute(value, axis, [(source, source + steps) for source in range(i...  3.69 us
    sub x1, other arithmetic, per_device(): adjoint = adjoint - ar_weights[lag_pos] * ahead  3.26 us
  transfers between devices with their start and end apart: 4, of which 0 were waited for; matrix products, arithmetic and copies ran while one was open for 12% of the time, Pallas kernels for 0%

commit v1 on v0

v1 whole, which is shorter than its diff:
```python
import functools
import math

import jax
import jax.numpy as jnp
from jax import lax
from jax.experimental import pallas as pl
from jax.experimental.pallas import tpu as pltpu
from jax.sharding import PartitionSpec as P

NLAG = 16
LAGMAX = 128
TILE = 128
STEP = 64
F32 = jnp.float32
BF16 = jnp.bfloat16


def kernel(
    n, ns, scale_time, scale_series, row_tile,
    lags_ref, mask_ref, panel_ref, s_hbm, f_hbm, w_ref,
    out_s, out_t, out_a,
    pbuf, sbuf, fbuf, g, tt, tsend, trecv, ext, err, hprev, hnext,
    crx, s1, yrx, s2, zrx, ar0, ar1, arc, ary, arz,
    psem, insem, hsem, tsem, csem, ysem, zsem, acsem, aysem, azsem,
):
    rows, cols = pbuf.shape
    nz = n // 4
    block = rows // n
    chunk = rows // nz
    width = cols // ns
    part = rows // 4
    me = lax.axis_index("tm")
    my_s = lax.axis_index("series")
    c = lax.rem(me, 2)
    y = lax.rem(lax.div(me, 2), 2)
    z = lax.div(me, 4)
    core_peer = {"tm": me + 1 - 2 * c}
    y_peer = {"tm": me + 2 - 4 * y}
    low = lax.rem(me, 4)
    has_prev = me > 0
    has_next = me < n - 1
    other = me - 1 + 2 * c
    has_other = jnp.logical_and(other >= 0, other < n)

    def z_peer(i):
        return {"tm": lax.rem(z + 1 + i, nz) * 4 + low}

    def s_peer(o):
        return {"series": lax.rem(my_s + o, ns)}

    def remote(src, dst, sem, target):
        return pltpu.make_async_remote_copy(
            src_ref=src, dst_ref=dst, send_sem=sem.at[0], recv_sem=sem.at[1],
            device_id=target, device_id_type=pl.DeviceIdType.MESH)

    barrier = pltpu.get_barrier_semaphore()

    def greet(target):
        pl.semaphore_signal(barrier, inc=1, device_id=target,
                            device_id_type=pl.DeviceIdType.MESH)

    greet(core_peer)
    greet(y_peer)
    for i in range(nz - 1):
        greet(z_peer(i))
    for o in range(1, ns):
        greet(s_peer(o))

    @pl.when(has_other)
    def _():
        greet({"tm": other})

    load_s = pltpu.make_async_copy(s_hbm, sbuf, insem.at[0])
    load_f = pltpu.make_async_copy(f_hbm, fbuf, insem.at[1])
    load_s.start()
    load_f.start()

    def col0(o):
        return pl.multiple_of(lax.rem(my_s + o, ns) * width, TILE)

    def panel_load(o, k):
        window = (pl.ds(k * part, part), pl.ds(col0(o), width))
        return pltpu.make_async_copy(
            panel_ref.at[window], pbuf.at[window], psem.at[o, k])

    order = list(range(1, ns)) + [0]
    for o in order:
        for k in range(4):
            panel_load(o, k).start()
    load_s.wait()
    load_f.wait()

    def tile(o, r0, first):
        r0 = pl.multiple_of(r0, row_tile)
        c0 = col0(o)
        s = sbuf[pl.ds(r0, row_tile), :]
        f = fbuf[pl.ds(c0, width), :]
        pred = lax.dot_general(s, f, (((1,), (1,)), ((), ())), preferred_element_type=F32)
        diff = pred - pbuf[pl.ds(r0, row_tile), pl.ds(c0, width)].astype(F32)
        mr, mc = lax.div(r0, TILE), lax.div(c0, TILE)
        pieces = []
        for a in range(row_tile // TILE):
            keep = jnp.concatenate(
                [jnp.full((TILE, TILE), mask_ref[mr + a, mc + b], jnp.int32)
                 for b in range(width // TILE)], axis=1) > 0
            pieces.append(jnp.where(keep, diff[a * TILE:(a + 1) * TILE], 0.0))
        res = jnp.concatenate(pieces, axis=0).astype(BF16)
        add = jnp.dot(res, f, preferred_element_type=F32)
        if first:
            g[pl.ds(r0, row_tile), :] = add
        else:
            g[pl.ds(r0, row_tile), :] += add
        tt[o] += lax.dot_general(s, res, (((0,), (0,)), ((), ())), preferred_element_type=F32)

    def tiles(o, start, count, first):
        def body(k, carry):
            tile(o, start + k * row_tile, first)
            return carry
        lax.fori_loop(0, count, body, 0)

    tt[...] = jnp.zeros_like(tt)
    to_next = remote(fbuf.at[pl.ds(cols - LAGMAX, LAGMAX)], hprev, hsem.at[0],
                     {"tm": lax.min(me + 1, n - 1)})
    to_prev = remote(fbuf.at[pl.ds(0, LAGMAX)], hnext, hsem.at[1],
                     {"tm": lax.max(me - 1, 0)})
    tcopies = []
    for o in range(1, ns):
        for k in range(4):
            panel_load(o, k).wait()
            tiles(o, k * part, part // row_tile, o == 1)
            if o == 1 and k == 0:
                base = 1 + 1 + (nz - 1) + (ns - 1)
                pl.semaphore_wait(barrier, base + has_other.astype(jnp.int32))

                @pl.when(has_next)
                def _():
                    to_next.start()

                @pl.when(has_prev)
                def _():
                    to_prev.start()
        tsend[o - 1] = tt[o].T
        copy = remote(tsend.at[o - 1], trecv.at[o - 1], tsem.at[o - 1], s_peer(o))
        copy.start()
        tcopies.append(copy)

    ext[pl.ds(LAGMAX, cols), :] = fbuf[...].astype(F32)

    @pl.when(has_next)
    def _():
        to_next.wait_send()
        to_prev.wait_recv()
        ext[pl.ds(LAGMAX + cols, LAGMAX), :] = hnext[...].astype(F32)

    @pl.when(jnp.logical_not(has_next))
    def _():
        ext[pl.ds(LAGMAX + cols, LAGMAX), :] = jnp.zeros((LAGMAX, w_ref.shape[1]), F32)

    @pl.when(has_prev)
    def _():
        to_prev.wait_send()
        to_next.wait_recv()
        ext[pl.ds(0, LAGMAX), :] = hprev[...].astype(F32)

    @pl.when(jnp.logical_not(has_prev))
    def _():
        ext[pl.ds(0, LAGMAX), :] = jnp.zeros((LAGMAX, w_ref.shape[1]), F32)

    lags = [lags_ref[j] for j in range(NLAG)]
    rank = w_ref.shape[1]

    def error_tile(t0):
        total = ext[pl.ds(t0 + LAGMAX, STEP), :]
        for j in range(NLAG):
            total = total - w_ref[pl.ds(j, 1), :] * ext[pl.ds(t0 + LAGMAX - lags[j], STEP), :]
        return total

    def prior_body(k, sums):
        t0 = pl.multiple_of(k * STEP, STEP)
        live = jnp.logical_or(has_prev, t0 >= LAGMAX).astype(F32)
        total = error_tile(t0)
        total = jnp.where(jnp.full(total.shape, live) > 0, total, 0.0)
        err[pl.ds(t0, STEP), :] = total
        new = []
        for j in range(NLAG):
            prod = total * ext[pl.ds(t0 + LAGMAX - lags[j], STEP), :]
            new.append(sums[j] + prod.reshape(STEP // 8, 8, rank).sum(axis=0))
        return tuple(new)

    sums = lax.fori_loop(0, cols // STEP, prior_body,
                         tuple(jnp.zeros((8, rank), F32) for _ in range(NLAG)))

    def tail_body(k, carry):
        t0 = pl.multiple_of(cols + k * STEP, STEP)
        total = error_tile(t0)
        live = jnp.full(total.shape, has_next.astype(F32))
        err[pl.ds(t0, STEP), :] = jnp.where(live > 0, total, 0.0)
        return carry

    ar0[...] = jnp.concatenate([s.sum(axis=0, keepdims=True) for s in sums], axis=0)
    ar_core = remote(ar0, arc, acsem, core_peer)
    ar_core.start()
    lax.fori_loop(0, LAGMAX // STEP, tail_body, 0)

    def core_copy(i):
        q = lax.rem(z + 1 + i, nz)
        return remote(g4.at[q, :, 1 - c], crx.at[i], csem.at[i], core_peer)

    def y_copy(i):
        return remote(s1.at[i, 1 - y], yrx.at[i], ysem.at[i], y_peer)

    def z_copy(i):
        return remote(s2.at[i], zrx.at[i], zsem.at[i], z_peer(i))

    g4 = g.reshape(nz, 2, 2, block, rank)

    def after_core(i):
        q = lax.rem(z + 1 + i, nz)
        core_copy(i).wait()
        for b in range(2):
            s1[i, b] = g4[q, b, c] + crx[i, b]
        y_copy(i).start()

    def after_y(i):
        y_copy(i).wait()
        s2[i] = s1[i, y] + yrx[i]
        if i < nz - 1:
            z_copy(i).start()

    ar_y = remote(ar1, ary, aysem, y_peer)
    az = [remote(arz.at[z], arz.at[z], azsem.at[i], z_peer(i)) for i in range(nz - 1)]
    for k in range(4):
        panel_load(0, k).wait()
    for i in range(nz):
        q = lax.rem(z + 1 + i, nz)
        tiles(0, q * chunk, chunk // row_tile, ns == 1)
        core_copy(i).start()
        if i == 0:
            ar_core.wait()
            ar1[...] = ar0[...] + arc[...]
            ar_y.start()
        if i >= 1:
            after_core(i - 1)
        if i == min(1, nz - 1):
            ar_y.wait()
            arz[z] = ar1[...] + ary[...]
            for copy in az:
                copy.start()
        if i >= 2:
            after_y(i - 2)
    if nz >= 2:
        after_y(nz - 2)
    after_core(nz - 1)

    own = tt[0].T
    tsend[ns - 1] = own
    for copy in tcopies:
        copy.wait()
    own0 = my_s * width

    def out_body(k, carry):
        t0 = pl.multiple_of(k * STEP, STEP)
        base = pl.multiple_of(own0 + t0, STEP)
        adj = err[pl.ds(base, STEP), :]
        for j in range(NLAG):
            adj = adj - w_ref[pl.ds(j, 1), :] * err[pl.ds(base + lags[j], STEP), :]
        data = tsend[ns - 1, pl.ds(t0, STEP), :]
        for o in range(1, ns):
            data = data + trecv[o - 1, pl.ds(t0, STEP), :]
        out_t[pl.ds(t0, STEP), :] = data * scale_series + adj
        return carry

    lax.fori_loop(0, width // STEP, out_body, 0)

    for copy in az:
        copy.wait()
    total = arz[0]
    for k in range(1, nz):
        total = total + arz[k]
    out_a[...] = total * (-scale_time)

    after_y(nz - 1)
    total = s2[nz - 1]
    for i in range(nz - 1):
        z_copy(i).wait()
        total = total + zrx[i]
    out_s[...] = total * scale_time


def per_device(panel, series_factors, time_factors, ar_weights, tile_mask, lags):
    rows, cols = panel.shape
    rank = series_factors.shape[1]
    n = lax.axis_size("tm")
    ns = lax.axis_size("series")
    nz = n // 4
    block = rows // n
    width = cols // ns
    row_tile = min(2 * TILE, rows // nz)
    any_space = pl.BlockSpec(memory_space=pl.ANY)
    smem = pl.BlockSpec(memory_space=pltpu.SMEM)
    vmem = pl.BlockSpec(memory_space=pltpu.VMEM)
    dma = pltpu.SemaphoreType.DMA
    body = functools.partial(
        kernel, n, ns, 1.0 / math.sqrt(cols * n), 1.0 / math.sqrt(rows * ns), row_tile)
    return pl.pallas_call(
        body,
        out_shape=(
            jax.ShapeDtypeStruct((block, rank), F32),
            jax.ShapeDtypeStruct((width, rank), F32),
            jax.ShapeDtypeStruct((NLAG, rank), F32),
        ),
        in_specs=[smem, smem, any_space, any_space, any_space, vmem],
        out_specs=(vmem, vmem, vmem),
        scratch_shapes=[
            pltpu.VMEM((rows, cols), BF16),
            pltpu.VMEM((rows, rank), BF16),
            pltpu.VMEM((cols, rank), BF16),
            pltpu.VMEM((rows, rank), F32),
            pltpu.VMEM((ns, rank, width), F32),
            pltpu.VMEM((ns, width, rank), F32),
            pltpu.VMEM((max(ns - 1, 1), width, rank), F32),
            pltpu.VMEM((cols + 2 * LAGMAX, rank), F32),
            pltpu.VMEM((cols + LAGMAX, rank), F32),
            pltpu.VMEM((LAGMAX, rank), BF16),
            pltpu.VMEM((LAGMAX, rank), BF16),
            pltpu.VMEM((nz, 2, block, rank), F32),
            pltpu.VMEM((nz, 2, block, rank), F32),
            pltpu.VMEM((nz, block, rank), F32),
            pltpu.VMEM((nz, block, rank), F32),
            pltpu.VMEM((max(nz - 1, 1), block, rank), F32),
            pltpu.VMEM((NLAG, rank), F32),
            pltpu.VMEM((NLAG, rank), F32),
            pltpu.VMEM((NLAG, rank), F32),
            pltpu.VMEM((NLAG, rank), F32),
            pltpu.VMEM((nz, NLAG, rank), F32),
            dma((ns, 4)),
            dma((2,)),
            dma((2, 2)),
            dma((max(ns - 1, 1), 2)),
            dma((nz, 2)),
            dma((nz, 2)),
            dma((max(nz - 1, 1), 2)),
            dma((2,)),
            dma((2,)),
            dma((max(nz - 1, 1), 2)),
        ],
        compiler_params=pltpu.CompilerParams(collective_id=0, has_side_effects=True),
        name="factor_grad",
    )(lags, tile_mask, panel, series_factors, time_factors, ar_weights)


def solution(mesh):
    in_specs = (P("series", "tm"), P("series", None), P("tm", None), P(), P("series", "tm"), P())
    out_specs = (P(("series", "tm"), None), P(("tm", "series"), None), P())
    return jax.shard_map(
        per_device, mesh=mesh, in_specs=in_specs, out_specs=out_specs, check_vma=False
    )
```

time: 139 us -> 32.3 us (0.23)
  between operations: 64.6 us -> 0.64 us
  blocking collectives: 37.2 us -> 0 us
  Pallas kernels: 0 us -> 25.5 us
  other arithmetic: 12.2 us -> 0 us
  matrix products: 10.6 us -> 0 us
  starting transfers between devices: 3.77 us -> 0 us
  local copies, waits for them, and re-layouts: 9.25 us -> 5.79 us
    psum x1 -> x0, blocking collectives: 37.2 us -> none  [per_device(): ar_grad = lax.psum(ar_part, 'tm')]
    pallas_call x0 -> x1, Pallas kernels: none -> 25.5 us  [per_device(): pl.pallas_call(body, out_shape=(jax.ShapeDtypeStruct((block, rank), F32),...]
    dot_general x3 -> x0, matrix products: 10.6 us -> none  [the longest x1 4.42 us: per_device(): jnp.dot(residual, time_factors, preferred_element_type=jnp.float32)]
    broadcast_in_dim x2 -> x0, local copies, waits for them, and re-layouts: 6.44 us -> none  [per_device(): keep = jnp.repeat(jnp.repeat(tile_mask, TILE, 0), TILE, 1) > 0]
    reduce_sum x3 -> x0, other arithmetic: 5.29 us -> none  [per_device(): ar_rows.append(-scale_time * jnp.sum(error * behind, axis=0))]
    unnamed x10 -> x4, local copies, waits for them, and re-layouts: 1.94 us -> 5.79 us
    ppermute x2 -> x0, starting transfers between devices: 3.69 us -> none  [from_behind(): lax.ppermute(value, axis, [(source, source + steps) for source in range(i...]
    sub x1 -> x0, other arithmetic: 3.26 us -> none  [per_device(): adjoint = adjoint - ar_weights[lag_pos] * ahead]
  transfers between devices with their start and end apart: 4 -> 0, of which waited for: 0 -> 0; matrix products, arithmetic and copies ran while one was open for 12% -> 0% of each run, Pallas kernels for 0% -> 0%
where the time goes in v1:
time: 32.3 us; the launch traced here: 32 us
  Pallas kernels  25.5 us (79%)
  local copies, waits for them, and re-layouts  5.79 us (18%)
  between operations  0.64 us (2%)
    pallas_call x1, Pallas kernels, per_device(): pl.pallas_call(body, out_shape=(jax.ShapeDtypeStruct((block, rank), F32),...  25.5 us
    unnamed x4, local copies, waits for them, and re-layouts  5.79 us

profile of v1, /device:TPU:0, one launch (start us, length us, event | category | flops | bytes accessed | tf_op | source)
XLA Modules:
  0.0 32.0 jit_solution(11069268326704402510)
XLA Ops:
  0.6 1.4 %copy.9.mask_ref = s32[16,8]{1,0:T(8,128)} copy(s32[16,8]{0,1:T(8,128)} %param.10) | data formatting | bytes 1024 | tf_op args[4]
  2.0 25.5 %factor_grad.1 = (f32[128,128]{1,0:T(8,128)}, f32[512,128]{1,0:T(8,128)}, f32[16,128]{1,0:T(8,128)}) custom-call(s32[16]{0:T(128)} %lags_ref.1, s32[16,8]{1,0:T(8,128)} %copy.9.mask_ref, bf16[2048,1024]{1,0:T(8,128)(2,1)} %panel_ref.1, bf16[2048,128]{1,0:T(8,128)(2,1)} %s_hbm.1, bf16[1024,128]{1,0:T(8,128)(2,1)} %f_hbm.1, f32[16,128]{1,0:T(8,128)} %w_ref.1), custom_call_target="tpu_custom_call" | custom-call | tf_op jit(solution)/shard_map/factor_grad/pallas_call | solution.py:306
  27.5 1.5 %copy.13 = f32[128,128]{1,0:T(8,128)} copy(f32[128,128]{1,0:T(8,128)} %get-tuple-element.6) | data formatting | bytes 131072
  29.0 1.7 %copy.14 = f32[512,128]{1,0:T(8,128)} copy(f32[512,128]{1,0:T(8,128)} %get-tuple-element.7) | data formatting | bytes 524288
  30.7 1.3 %copy.15 = f32[16,128]{1,0:T(8,128)} copy(f32[16,128]{1,0:T(8,128)} %get-tuple-element.8) | data formatting | bytes 16384

commit v2 on v1

v2 whole, which is shorter than its diff:
```python
import functools
import math

import jax
import jax.numpy as jnp
from jax import lax
from jax.experimental import pallas as pl
from jax.experimental.pallas import tpu as pltpu
from jax.sharding import PartitionSpec as P

NLAG = 16
LAGMAX = 128
TILE = 128
STEP = 64
F32 = jnp.float32
BF16 = jnp.bfloat16


def kernel(
    n, ns, scale_time, scale_series, row_tile,
    lags_hbm, mask_hbm, panel_ref, s_hbm, f_hbm, w_hbm,
    out_s, out_t, out_a,
    lags_ref, mask_ref, w_ref, pbuf, sbuf, fbuf, g, tt, tsend, own, trecv, ext, err, hprev, hnext,
    crx, s1, yrx, s2, zrx, ar0, ar1, arc, ary, arz,
    psem, insem, hsem, tsem, csem, ysem, zsem, acsem, aysem, azsem,
):
    rows, cols = pbuf.shape
    nz = n // 4
    block = rows // n
    chunk = rows // nz
    width = cols // ns
    me = lax.axis_index("tm")
    my_s = lax.axis_index("series")
    c = lax.rem(me, 2)
    y = lax.rem(lax.div(me, 2), 2)
    z = lax.div(me, 4)
    core_peer = {"tm": me + 1 - 2 * c}
    y_peer = {"tm": me + 2 - 4 * y}
    low = lax.rem(me, 4)
    has_prev = me > 0
    has_next = me < n - 1
    other = me - 1 + 2 * c
    has_other = jnp.logical_and(other >= 0, other < n)

    def z_peer(i):
        return {"tm": lax.rem(z + 1 + i, nz) * 4 + low}

    def s_peer(o):
        return {"series": lax.rem(my_s + o, ns)}

    def remote(src, dst, sem, target):
        return pltpu.make_async_remote_copy(
            src_ref=src, dst_ref=dst, send_sem=sem.at[0], recv_sem=sem.at[1],
            device_id=target, device_id_type=pl.DeviceIdType.MESH)

    barrier = pltpu.get_barrier_semaphore()

    def greet(target):
        pl.semaphore_signal(barrier, inc=1, device_id=target,
                            device_id_type=pl.DeviceIdType.MESH)

    greet(core_peer)
    greet(y_peer)
    for i in range(nz - 1):
        greet(z_peer(i))
    for o in range(1, ns):
        greet(s_peer(o))

    @pl.when(has_other)
    def _():
        greet({"tm": other})

    loads = [pltpu.make_async_copy(a, b, insem.at[k]) for k, (a, b) in enumerate(
        [(s_hbm, sbuf), (f_hbm, fbuf), (mask_hbm, mask_ref), (w_hbm, w_ref), (lags_hbm, lags_ref)])]

    def place(i):
        return lax.rem(z + 1 + i, nz)

    def panel_load(i):
        window = (pl.ds(place(i) * chunk, chunk), slice(None))
        return pltpu.make_async_copy(panel_ref.at[window], pbuf.at[window], psem.at[i])

    for k in range(3):
        loads[k].start()
    panel_load(0).start()
    loads[3].start()
    loads[4].start()
    for i in range(1, nz):
        panel_load(i).start()
    tt[...] = jnp.zeros_like(tt)
    for k in range(3):
        loads[k].wait()

    def tile(r0):
        r0 = pl.multiple_of(r0, row_tile)
        s = sbuf[pl.ds(r0, row_tile), :]
        f = fbuf[...]
        mr = lax.div(r0, TILE)
        pred = lax.dot_general(s, f, (((1,), (1,)), ((), ())), preferred_element_type=F32)
        diff = pred - pbuf[pl.ds(r0, row_tile), :].astype(F32)
        pieces = []
        for a in range(row_tile // TILE):
            keep = jnp.concatenate(
                [jnp.full((TILE, TILE), mask_ref[b, mr + a], jnp.int32)
                 for b in range(cols // TILE)], axis=1) > 0
            pieces.append(jnp.where(keep, diff[a * TILE:(a + 1) * TILE], 0.0))
        res = jnp.concatenate(pieces, axis=0).astype(BF16)
        g[pl.ds(r0, row_tile), :] = jnp.dot(res, f, preferred_element_type=F32)
        add = lax.dot_general(s, res, (((0,), (0,)), ((), ())), preferred_element_type=F32)
        for k in range(ns):
            tt[k] += add[:, k * width:(k + 1) * width]

    def tiles(i):
        start = place(i) * chunk
        panel_load(i).wait()

        def body(k, carry):
            tile(start + k * row_tile)
            return carry
        lax.fori_loop(0, chunk // row_tile, body, 0)

    to_next = remote(fbuf.at[pl.ds(cols - LAGMAX, LAGMAX)], hprev, hsem.at[0],
                     {"tm": lax.min(me + 1, n - 1)})
    to_prev = remote(fbuf.at[pl.ds(0, LAGMAX)], hnext, hsem.at[1],
                     {"tm": lax.max(me - 1, 0)})
    rank = w_ref.shape[1]
    g4 = g.reshape(nz, 2, 2, block, rank)

    def core_copy(i):
        return remote(g4.at[place(i), :, 1 - c], crx.at[i], csem.at[i], core_peer)

    def y_copy(i):
        return remote(s1.at[i, 1 - y], yrx.at[i], ysem.at[i], y_peer)

    def z_copy(i):
        return remote(s2.at[i], zrx.at[i], zsem.at[i], z_peer(i))

    def after_core(i):
        core_copy(i).wait()
        for b in range(2):
            s1[i, b] = g4[place(i), b, c] + crx[i, b]
        y_copy(i).start()

    def after_y(i):
        y_copy(i).wait()
        s2[i] = s1[i, y] + yrx[i]
        if i < nz - 1:
            z_copy(i).start()

    tcopies = [remote(tsend.at[o - 1], trecv.at[o - 1], tsem.at[o - 1], s_peer(o))
               for o in range(1, ns)]
    ar_core = remote(ar0, arc, acsem, core_peer)
    ar_y = remote(ar1, ary, aysem, y_peer)
    az = [remote(arz.at[z], arz.at[z], azsem.at[i], z_peer(i)) for i in range(nz - 1)]

    def error_tile(t0, lags):
        total = ext[pl.ds(t0 + LAGMAX, STEP), :]
        for j in range(NLAG):
            total = total - w_ref[pl.ds(j, 1), :] * ext[pl.ds(t0 + LAGMAX - lags[j], STEP), :]
        return total

    def all_lags():
        return [lags_ref[j] for j in range(NLAG)]

    def prior_start():
        loads[3].wait()
        loads[4].wait()
        ext[pl.ds(LAGMAX, cols), :] = fbuf[...].astype(F32)
        blank = jnp.zeros((LAGMAX, rank), F32)

        @pl.when(has_next)
        def _():
            to_next.wait_send()
            to_prev.wait_recv()
            ext[pl.ds(LAGMAX + cols, LAGMAX), :] = hnext[...].astype(F32)

        @pl.when(jnp.logical_not(has_next))
        def _():
            ext[pl.ds(LAGMAX + cols, LAGMAX), :] = blank

        @pl.when(has_prev)
        def _():
            to_prev.wait_send()
            to_next.wait_recv()
            ext[pl.ds(0, LAGMAX), :] = hprev[...].astype(F32)

        @pl.when(jnp.logical_not(has_prev))
        def _():
            ext[pl.ds(0, LAGMAX), :] = blank

        lags = all_lags()

        def body(k, sums):
            t0 = pl.multiple_of(k * STEP, STEP)
            live = jnp.logical_or(has_prev, t0 >= LAGMAX).astype(F32)
            total = error_tile(t0, lags)
            total = jnp.where(jnp.full(total.shape, live) > 0, total, 0.0)
            err[pl.ds(t0, STEP), :] = total
            new = []
            for j in range(NLAG):
                prod = total * ext[pl.ds(t0 + LAGMAX - lags[j], STEP), :]
                new.append(sums[j] + prod.reshape(STEP // 8, 8, rank).sum(axis=0))
            return tuple(new)

        sums = lax.fori_loop(0, cols // STEP, body,
                             tuple(jnp.zeros((8, rank), F32) for _ in range(NLAG)))
        ar0[...] = jnp.concatenate([s.sum(axis=0, keepdims=True) for s in sums], axis=0)
        ar_core.start()

    def adjoint():
        lags = all_lags()

        def tail(k, carry):
            t0 = pl.multiple_of(cols + k * STEP, STEP)
            total = error_tile(t0, lags)
            live = jnp.full(total.shape, has_next.astype(F32))
            err[pl.ds(t0, STEP), :] = jnp.where(live > 0, total, 0.0)
            return carry

        def body(k, carry):
            t0 = pl.multiple_of(k * STEP, STEP)
            base = pl.multiple_of(my_s * width + t0, STEP)
            adj = err[pl.ds(base, STEP), :]
            for j in range(NLAG):
                adj = adj - w_ref[pl.ds(j, 1), :] * err[pl.ds(base + lags[j], STEP), :]
            own[pl.ds(t0, STEP), :] += adj
            return carry

        lax.fori_loop(0, LAGMAX // STEP, tail, 0)
        lax.fori_loop(0, width // STEP, body, 0)

    for i in range(nz):
        if i == nz - 1:
            prior_start()
            if i >= 1:
                after_core(i - 1)
        tiles(i)
        if i == 0:
            base = 1 + 1 + (nz - 1) + (ns - 1)
            pl.semaphore_wait(barrier, base + has_other.astype(jnp.int32))

            @pl.when(has_next)
            def _():
                to_next.start()

            @pl.when(has_prev)
            def _():
                to_prev.start()
        core_copy(i).start()
        if i == nz - 1:
            for o in range(1, ns):
                tsend[o - 1] = tt[lax.rem(my_s + o, ns)].T
                tcopies[o - 1].start()
        elif i >= 1:
            after_core(i - 1)
        if i >= 3:
            after_y(i - 3)
    ar_core.wait()
    ar1[...] = ar0[...] + arc[...]
    ar_y.start()
    after_core(nz - 1)
    if nz >= 3:
        after_y(nz - 3)
    own[...] = tt[my_s].T * scale_series
    adjoint()
    if nz >= 2:
        after_y(nz - 2)
    ar_y.wait()
    arz[z] = ar1[...] + ary[...]
    for copy in az:
        copy.start()
    after_y(nz - 1)
    for copy in tcopies:
        copy.wait()
    data = own[...]
    for o in range(1, ns):
        data = data + trecv[o - 1] * scale_series
    out_t[...] = data
    for copy in az:
        copy.wait()
    total = arz[0]
    for k in range(1, nz):
        total = total + arz[k]
    out_a[...] = total * (-scale_time)
    total = s2[nz - 1]
    for i in range(nz - 1):
        z_copy(i).wait()
        total = total + zrx[i]
    out_s[...] = total * scale_time


def put_out(*refs):
    sem = refs[-1]
    copies = [pltpu.make_async_copy(refs[k], refs[3 + k], sem.at[k]) for k in range(3)]
    for copy in copies:
        copy.start()
    for copy in copies:
        copy.wait()


def per_device(panel, series_factors, time_factors, ar_weights, tile_mask, lags):
    rows, cols = panel.shape
    rank = series_factors.shape[1]
    n = lax.axis_size("tm")
    ns = lax.axis_size("series")
    nz = n // 4
    block = rows // n
    width = cols // ns
    row_tile = min(2 * TILE, rows // nz)
    any_space = pl.BlockSpec(memory_space=pl.ANY)
    vmem = pl.BlockSpec(memory_space=pltpu.VMEM)
    dma = pltpu.SemaphoreType.DMA
    body = functools.partial(
        kernel, n, ns, 1.0 / math.sqrt(cols * n), 1.0 / math.sqrt(rows * ns), row_tile)
    shapes = ((block, rank), (width, rank), (NLAG, rank))
    results = pl.pallas_call(
        body,
        out_shape=tuple(pltpu.VMEM(shape, F32) for shape in shapes),
        in_specs=[any_space] * 6,
        out_specs=(vmem, vmem, vmem),
        scratch_shapes=[
            pltpu.SMEM((NLAG,), jnp.int32),
            pltpu.SMEM(tile_mask.shape[::-1], jnp.int32),
            pltpu.VMEM((NLAG, rank), F32),
            pltpu.VMEM((rows, cols), BF16),
            pltpu.VMEM((rows, rank), BF16),
            pltpu.VMEM((cols, rank), BF16),
            pltpu.VMEM((rows, rank), F32),
            pltpu.VMEM((ns, rank, width), F32),
            pltpu.VMEM((max(ns - 1, 1), width, rank), F32),
            pltpu.VMEM((width, rank), F32),
            pltpu.VMEM((max(ns - 1, 1), width, rank), F32),
            pltpu.VMEM((cols + 2 * LAGMAX, rank), F32),
            pltpu.VMEM((cols + LAGMAX, rank), F32),
            pltpu.VMEM((LAGMAX, rank), BF16),
            pltpu.VMEM((LAGMAX, rank), BF16),
            pltpu.VMEM((nz, 2, block, rank), F32),
            pltpu.VMEM((nz, 2, block, rank), F32),
            pltpu.VMEM((nz, block, rank), F32),
            pltpu.VMEM((nz, block, rank), F32),
            pltpu.VMEM((max(nz - 1, 1), block, rank), F32),
            pltpu.VMEM((NLAG, rank), F32),
            pltpu.VMEM((NLAG, rank), F32),
            pltpu.VMEM((NLAG, rank), F32),
            pltpu.VMEM((NLAG, rank), F32),
            pltpu.VMEM((nz, NLAG, rank), F32),
            dma((nz,)),
            dma((5,)),
            dma((2, 2)),
            dma((max(ns - 1, 1), 2)),
            dma((nz, 2)),
            dma((nz, 2)),
            dma((max(nz - 1, 1), 2)),
            dma((2,)),
            dma((2,)),
            dma((max(nz - 1, 1), 2)),
        ],
        compiler_params=pltpu.CompilerParams(collective_id=0, has_side_effects=True),
        name="factor_grad",
    )(lags, tile_mask.T, panel, series_factors, time_factors, ar_weights)
    return pl.pallas_call(
        put_out,
        out_shape=tuple(jax.ShapeDtypeStruct(shape, F32) for shape in shapes),
        in_specs=[vmem] * 3,
        out_specs=(any_space,) * 3,
        scratch_shapes=[dma((3,))],
        name="put_out",
    )(*[pltpu.with_memory_space_constraint(r, pltpu.VMEM) for r in results])


def solution(mesh):
    in_specs = (P("series", "tm"), P("series", None), P("tm", None), P(), P("series", "tm"), P())
    out_specs = (P(("series", "tm"), None), P(("tm", "series"), None), P())
    return jax.shard_map(
        per_device, mesh=mesh, in_specs=in_specs, out_specs=out_specs, check_vma=False
    )
```

time: 32.3 us -> 22.6 us (0.70)
  local copies, waits for them, and re-layouts: 5.79 us -> 0 us
  Pallas kernels: 25.5 us -> 21.8 us
    unnamed x4 -> x0, local copies, waits for them, and re-layouts: 5.79 us -> none
    pallas_call x1 -> x2, Pallas kernels: 25.5 us -> 21.8 us  [the longest x1 21.1 us: per_device(): pl.pallas_call(body, out_shape=tuple((pltpu.VMEM(shape, F32) for shape in...]
where the time goes in v2:
time: 22.6 us; the launch traced here: 22.4 us
  Pallas kernels  21.8 us (96%)
  between operations  0.64 us (3%)
    pallas_call x1, Pallas kernels, per_device(): pl.pallas_call(body, out_shape=tuple((pltpu.VMEM(shape, F32) for shape in...  21.1 us
    pallas_call x1, Pallas kernels, per_device(): pl.pallas_call(put_out, out_shape=tuple((jax.ShapeDtypeStruct(shape, F32)...  0.75 us

profile of v2, /device:TPU:0, one launch (start us, length us, event | category | flops | bytes accessed | tf_op | source)
XLA Modules:
  0.0 22.4 jit_solution(5085703395174103065)
XLA Ops:
  0.6 21.1 %factor_grad.1 = (f32[128,128]{1,0:T(8,128)S(1)}, f32[512,128]{1,0:T(8,128)S(1)}, f32[16,128]{1,0:T(8,128)S(1)}) custom-call(s32[16]{0:T(128)} %lags_hbm.1, s32[8,16]{1,0:T(8,128)} %bitcast.1, bf16[2048,1024]{1,0:T(8,128)(2,1)} %panel_ref.1, bf16[2048,128]{1,0:T(8,128)(2,1)} %s_hbm.1, bf16[1024,128]{1,0:T(8,128)(2,1)} %f_hbm.1, f32[16,128]{1,0:T(8,128)} %w_hbm.1), custom_call_target="tpu_custom_call" | custom-call | tf_op jit(solution)/shard_map/factor_grad/pallas_call | solution.py:316
  21.7 0.8 %put_out.1 = (f32[128,128]{1,0:T(8,128)}, f32[512,128]{1,0:T(8,128)}, f32[16,128]{1,0:T(8,128)}) custom-call(f32[128,128]{1,0:T(8,128)S(1)} %get-tuple-element.6.refs_0_, f32[512,128]{1,0:T(8,128)S(1)} %get-tuple-element.7.refs_1_, f32[16,128]{1,0:T(8,128)S(1)} %get-tuple-element.8.refs_2_), custom_call_target="tpu_custom_call" | custom-call | tf_op jit(solution)/shard_map/put_out/pallas_call | solution.py:361

commit v3 on v2

--- a/solution.py
+++ b/solution.py
@@ -16,13 +16,26 @@
 BF16 = jnp.bfloat16
 
 
+LEVELS = 32767.0
+
+
+def code(value):
+    top = jnp.maximum(jnp.max(jnp.abs(value), axis=0, keepdims=True), 1e-30)
+    levels = jnp.round(value * (LEVELS / top)).astype(jnp.int32).astype(jnp.int16)
+    return levels, jnp.broadcast_to(top * (1.0 / LEVELS), (8, value.shape[1]))
+
+
+def decode(levels, step):
+    return levels.astype(jnp.int32).astype(F32) * step[0:1]
+
+
 def kernel(
     n, ns, scale_time, scale_series, row_tile,
     lags_hbm, mask_hbm, panel_ref, s_hbm, f_hbm, w_hbm,
     out_s, out_t, out_a,
-    lags_ref, mask_ref, w_ref, pbuf, sbuf, fbuf, g, tt, tsend, own, trecv, ext, err, hprev, hnext,
-    crx, s1, yrx, s2, zrx, ar0, ar1, arc, ary, arz,
-    psem, insem, hsem, tsem, csem, ysem, zsem, acsem, aysem, azsem,
+    lags_ref, mask_ref, w_ref, pbuf, sbuf, fbuf, g, tt, tsend, tstep, own, trecv, trstep, ext, err, hprev, hnext,
+    crx, s1, ysend, ystep, yrx, yrstep, s2, zsend, zstep, zrx, zrstep, ar0, ar1, arc, ary, arz,
+    psem, insem, hsem, tsem, csem, ysem, zsem, tsem2, ysem2, zsem2, acsem, aysem, azsem,
 ):
     rows, cols = pbuf.shape
     nz = n // 4
@@ -129,26 +142,37 @@
     def core_copy(i):
         return remote(g4.at[place(i), :, 1 - c], crx.at[i], csem.at[i], core_peer)
 
+    def both(levels, step, lrecv, srecv, lsem, ssem, target):
+        return (remote(levels, lrecv, lsem, target), remote(step, srecv, ssem, target))
+
     def y_copy(i):
-        return remote(s1.at[i, 1 - y], yrx.at[i], ysem.at[i], y_peer)
+        return both(ysend.at[i], ystep.at[i], yrx.at[i], yrstep.at[i],
+                    ysem.at[i], ysem2.at[i], y_peer)
 
     def z_copy(i):
-        return remote(s2.at[i], zrx.at[i], zsem.at[i], z_peer(i))
+        return both(zsend.at[i], zstep.at[i], zrx.at[i], zrstep.at[i],
+                    zsem.at[i], zsem2.at[i], z_peer(i))
 
     def after_core(i):
         core_copy(i).wait()
-        for b in range(2):
-            s1[i, b] = g4[place(i), b, c] + crx[i, b]
-        y_copy(i).start()
+        ysend[i], ystep[i] = code(g4[place(i), 1 - y, c] + crx[i, 1 - y])
+        for copy in y_copy(i):
+            copy.start()
+        s1[i] = g4[place(i), y, c] + crx[i, y]
 
     def after_y(i):
-        y_copy(i).wait()
-        s2[i] = s1[i, y] + yrx[i]
+        for copy in y_copy(i):
+            copy.wait()
+        total = s1[i] + decode(yrx[i], yrstep[i])
         if i < nz - 1:
-            z_copy(i).start()
-
-    tcopies = [remote(tsend.at[o - 1], trecv.at[o - 1], tsem.at[o - 1], s_peer(o))
-               for o in range(1, ns)]
+            zsend[i], zstep[i] = code(total)
+            for copy in z_copy(i):
+                copy.start()
+        else:
+            s2[...] = total
+
+    tcopies = [both(tsend.at[o - 1], tstep.at[o - 1], trecv.at[o - 1], trstep.at[o - 1],
+                    tsem.at[o - 1], tsem2.at[o - 1], s_peer(o)) for o in range(1, ns)]
     ar_core = remote(ar0, arc, acsem, core_peer)
     ar_y = remote(ar1, ary, aysem, y_peer)
     az = [remote(arz.at[z], arz.at[z], azsem.at[i], z_peer(i)) for i in range(nz - 1)]
@@ -249,8 +273,11 @@
         core_copy(i).start()
         if i == nz - 1:
             for o in range(1, ns):
-                tsend[o - 1] = tt[lax.rem(my_s + o, ns)].T
-                tcopies[o - 1].start()
+                value = tt[lax.rem(my_s + o, ns)].T
+                for k in range(width // TILE):
+                    tsend[o - 1, k], tstep[o - 1, k] = code(value[k * TILE:(k + 1) * TILE])
+                for copy in tcopies[o - 1]:
+                    copy.start()
         elif i >= 1:
             after_core(i - 1)
         if i >= 3:
@@ -270,22 +297,25 @@
     for copy in az:
         copy.start()
     after_y(nz - 1)
-    for copy in tcopies:
-        copy.wait()
-    data = own[...]
-    for o in range(1, ns):
-        data = data + trecv[o - 1] * scale_series
-    out_t[...] = data
+    for copies in tcopies:
+        for copy in copies:
+            copy.wait()
+    for k in range(width // TILE):
+        data = own[pl.ds(k * TILE, TILE), :]
+        for o in range(1, ns):
+            data = data + decode(trecv[o - 1, k], trstep[o - 1, k]) * scale_series
+        out_t[pl.ds(k * TILE, TILE), :] = data
     for copy in az:
         copy.wait()
     total = arz[0]
     for k in range(1, nz):
         total = total + arz[k]
     out_a[...] = total * (-scale_time)
-    total = s2[nz - 1]
+    total = s2[...]
     for i in range(nz - 1):
-        z_copy(i).wait()
-        total = total + zrx[i]
+        for copy in z_copy(i):
+            copy.wait()
+        total = total + decode(zrx[i], zrstep[i])
     out_s[...] = total * scale_time
 
 
@@ -327,18 +357,26 @@
             pltpu.VMEM((cols, rank), BF16),
             pltpu.VMEM((rows, rank), F32),
             pltpu.VMEM((ns, rank, width), F32),
-            pltpu.VMEM((max(ns - 1, 1), width, rank), F32),
+            pltpu.VMEM((max(ns - 1, 1), width // TILE, TILE, rank), jnp.int16),
+            pltpu.VMEM((max(ns - 1, 1), width // TILE, 8, rank), F32),
             pltpu.VMEM((width, rank), F32),
-            pltpu.VMEM((max(ns - 1, 1), width, rank), F32),
+            pltpu.VMEM((max(ns - 1, 1), width // TILE, TILE, rank), jnp.int16),
+            pltpu.VMEM((max(ns - 1, 1), width // TILE, 8, rank), F32),
             pltpu.VMEM((cols + 2 * LAGMAX, rank), F32),
             pltpu.VMEM((cols + LAGMAX, rank), F32),
             pltpu.VMEM((LAGMAX, rank), BF16),
             pltpu.VMEM((LAGMAX, rank), BF16),
             pltpu.VMEM((nz, 2, block, rank), F32),
-            pltpu.VMEM((nz, 2, block, rank), F32),
             pltpu.VMEM((nz, block, rank), F32),
-            pltpu.VMEM((nz, block, rank), F32),
-            pltpu.VMEM((max(nz - 1, 1), block, rank), F32),
+            pltpu.VMEM((nz, block, rank), jnp.int16),
+            pltpu.VMEM((nz, 8, rank), F32),
+            pltpu.VMEM((nz, block, rank), jnp.int16),
+            pltpu.VMEM((nz, 8, rank), F32),
+            pltpu.VMEM((block, rank), F32),
+            pltpu.VMEM((max(nz - 1, 1), block, rank), jnp.int16),
+            pltpu.VMEM((max(nz - 1, 1), 8, rank), F32),
+            pltpu.VMEM((max(nz - 1, 1), block, rank), jnp.int16),
+            pltpu.VMEM((max(nz - 1, 1), 8, rank), F32),
             pltpu.VMEM((NLAG, rank), F32),
             pltpu.VMEM((NLAG, rank), F32),
             pltpu.VMEM((NLAG, rank), F32),
@@ -349,6 +387,9 @@
             dma((2, 2)),
             dma((max(ns - 1, 1), 2)),
             dma((nz, 2)),
+            dma((nz, 2)),
+            dma((max(nz - 1, 1), 2)),
+            dma((max(ns - 1, 1), 2)),
             dma((nz, 2)),
             dma((max(nz - 1, 1), 2)),
             dma((2,)),

time: 22.6 us -> 20.4 us (0.903)
  Pallas kernels: 21.8 us -> 19.6 us
    pallas_call x1, Pallas kernels: 21.1 us -> 18.9 us  [per_device(): pl.pallas_call(body, out_shape=tuple((pltpu.VMEM(shape, F32) for shape in...]
where the time goes in v3:
time: 20.4 us; the launch traced here: 20.2 us
  Pallas kernels  19.6 us (96%)
  between operations  0.64 us (3%)
    pallas_call x1, Pallas kernels, per_device(): pl.pallas_call(body, out_shape=tuple((pltpu.VMEM(shape, F32) for shape in...  18.9 us
    pallas_call x1, Pallas kernels, per_device(): pl.pallas_call(put_out, out_shape=tuple((jax.ShapeDtypeStruct(shape, F32)...  0.75 us

profile of v3, /device:TPU:0, one launch (start us, length us, event | category | flops | bytes accessed | tf_op | source)
XLA Modules:
  0.0 20.2 jit_solution(10990550280892508654)
XLA Ops:
  0.6 18.9 %factor_grad.1 = (f32[128,128]{1,0:T(8,128)S(1)}, f32[512,128]{1,0:T(8,128)S(1)}, f32[16,128]{1,0:T(8,128)S(1)}) custom-call(s32[16]{0:T(128)} %lags_hbm.1, s32[8,16]{1,0:T(8,128)} %bitcast.1, bf16[2048,1024]{1,0:T(8,128)(2,1)} %panel_ref.1, bf16[2048,128]{1,0:T(8,128)(2,1)} %s_hbm.1, bf16[1024,128]{1,0:T(8,128)(2,1)} %f_hbm.1, f32[16,128]{1,0:T(8,128)} %w_hbm.1), custom_call_target="tpu_custom_call" | custom-call | tf_op jit(solution)/shard_map/factor_grad/pallas_call | solution.py:346
  19.5 0.8 %put_out.1 = (f32[128,128]{1,0:T(8,128)}, f32[512,128]{1,0:T(8,128)}, f32[16,128]{1,0:T(8,128)}) custom-call(f32[128,128]{1,0:T(8,128)S(1)} %get-tuple-element.6.refs_0_, f32[512,128]{1,0:T(8,128)S(1)} %get-tuple-element.7.refs_1_, f32[16,128]{1,0:T(8,128)S(1)} %get-tuple-element.8.refs_2_), custom_call_target="tpu_custom_call" | custom-call | tf_op jit(solution)/shard_map/put_out/pallas_call | solution.py:402
